TPU v7x, 128 devices: a whole 4x4x4 slice. The times are simulated.
128 devices in a mesh: dp: 32 (over x, z, core), mp: 4 (over y).
Axes of the slice: x: 4, y: 4, z: 4, core: 2. Of those that a mesh axis runs over, the one named last changes fastest.
Arguments:
- tokens: bfloat16 [32, 768, 1536], P('dp'), may hold values from -6 to 6
- lengths: int32 [32], P('dp'), may hold values from 1 to 768, as said below
- buckets: int32 [32], P('dp'), may hold values from 0 to 3, as said below
- out_cotangent: bfloat16 [32, 768, 1536], P('dp'), may hold values from -6 to 6
- gain_attn: bfloat16 [1536], replicated, may hold values from 0.5 to 1.5
- w_query: bfloat16 [1536, 1536], P(None, 'mp'), may hold values from -0.15625 to 0.15625
- w_key: bfloat16 [1536, 1536], P(None, 'mp'), may hold values from -0.15625 to 0.15625
- w_value: bfloat16 [1536, 1536], P(None, 'mp'), may hold values from -0.15625 to 0.15625
- w_outgate: bfloat16 [1536, 1536], P(None, 'mp'), may hold values from -0.15625 to 0.15625
- w_forget: bfloat16 [1536, 24], P(None, 'mp'), may hold values from -0.15625 to 0.15625
- b_forget: bfloat16 [24], P('mp'), may hold values from 1 to 7
- w_out: bfloat16 [1536, 1536], P('mp'), may hold values from -1.5 to 1.5
- gain_mlp: bfloat16 [1536], replicated, may hold values from 0.5 to 1.5
- w_gate: bfloat16 [1536, 4096], P(None, 'mp'), may hold values from -0.15625 to 0.15625
- w_up: bfloat16 [1536, 4096], P(None, 'mp'), may hold values from -0.15625 to 0.15625
- w_down: bfloat16 [4096, 1536], P('mp'), may hold values from -0.09375 to 0.09375
Outputs:
- output: bfloat16 [32, 768, 1536], P('dp')
- input_grad: float32 [32, 768, 1536], P('dp')
- grad_gain_attn: float32 [1536], P('dp')
- grad_query: float32 [1536, 1536], P('dp', 'mp')
- grad_key: float32 [1536, 1536], P('dp', 'mp')
- grad_value: float32 [1536, 1536], P('dp', 'mp')
- grad_outgate: float32 [1536, 1536], P('dp', 'mp')
- grad_forget: float32 [1536, 24], P('dp', 'mp')
- grad_bias: float32 [24], P('mp')
- grad_out: float32 [1536, 1536], P('mp', 'dp')
- grad_gain_mlp: float32 [1536], P('dp')
- grad_gate: float32 [1536, 4096], P('dp', 'mp')
- grad_up: float32 [1536, 4096], P('dp', 'mp')
- grad_down: float32 [4096, 1536], P('mp', 'dp')
- rms: float32 [3, 4], replicated
Inputs may be any that keep to these rules, and one draw needn't show every extreme that they name: `lengths`: A sequence with bucket id b has a length between b * 192 + 1 and (b + 1) * 192; some sequence has length 768. `buckets`: every bucket id occurs in every draw.
All inputs are finite; a program needn't handle non-finite values.
Results may differ from a plain program's by a relative error of at most 0.014.
Values sent between devices are 32-bit elements; how exact they have to be, the bound alone decides.
A program may use at most 256 MiB of HBM per device.

v0:
```python
import math
import jax
import jax.numpy as jnp
from jax import lax
from jax.sharding import PartitionSpec as P

NBUCKET = 4
EPSILON = 1e-06


def sent_together(arrays, axis, dim, along):
    widths = [math.prod(a.shape[along:]) for a in arrays]
    both = jnp.concatenate(
        [a.reshape(*a.shape[:along], w) for a, w in zip(arrays, widths)], axis=along
    )
    filled = lax.psum_scatter(both, axis, scatter_dimension=dim, tiled=True)
    tiles = jnp.split(filled, [sum(widths[:k]) for k in range(1, len(widths))], axis=along)
    return tuple(
        (b.reshape(*filled.shape[:along], *a.shape[along:]) for a, b in zip(arrays, tiles))
    )


def side_by_side(arrays, axis, dim, along):
    both = jnp.concatenate(arrays, axis=along)
    filled, at, done = (lax.psum_scatter(both, axis, scatter_dimension=dim, tiled=True), 0, [])
    for a in arrays:
        done.append(lax.slice_in_dim(filled, at, at + a.shape[along], axis=along))
        at += a.shape[along]
    return tuple(done)


def sent_to_all(array, axis):
    devices = lax.axis_size(axis)
    return lax.all_to_all(
        jnp.broadcast_to(array[None], (devices, *array.shape)), axis, 0, 0, tiled=True
    )


def over_copies(array, axis):
    return sent_to_all(array, axis).sum(axis=0)


def in_one(arrays, axis):
    ends = [0]
    for a in arrays:
        ends.append(ends[-1] + a.size)
    subtotal = over_copies(jnp.concatenate([a.ravel() for a in arrays]), axis)
    return tuple((subtotal[b:e].reshape(a.shape) for a, b, e in zip(arrays, ends, ends[1:])))


def norm_rows(values):
    return values * lax.rsqrt(jnp.mean(values * values, axis=-1, keepdims=True) + EPSILON)


def gain_norm(values, gain_row):
    return norm_rows(values) * gain_row


def swiglu(gate_pre, up_pre):
    return jax.nn.silu(gate_pre) * up_pre


def low_dot(left, right):
    return jnp.dot(left, right, preferred_element_type=jnp.float32)


def back_dot(left, right):
    return lax.dot_general(
        left, right, (((0,), (0,)), ((), ())), preferred_element_type=jnp.float32
    )


def trans_dot(left, right):
    return lax.dot_general(
        left, right, (((1,), (1,)), ((), ())), preferred_element_type=jnp.float32
    )


def per_device(
    tokens,
    lengths,
    buckets,
    out_cotangent,
    gain_attn,
    w_query,
    w_key,
    w_value,
    w_outgate,
    w_forget,
    b_forget,
    w_out,
    gain_mlp,
    w_gate,
    w_up,
    w_down,
):
    inputs = tokens[0].astype(jnp.float32)
    seq_len, model_width = inputs.shape
    head_count = w_forget.shape[1]
    head_dim = w_query.shape[1] // head_count
    score_scale = head_dim ** (-0.5)
    valid_len = lengths[0]
    positions = jnp.arange(seq_len)
    valid_rows = (positions < valid_len).astype(jnp.float32)[:, None]
    allowed = (positions[None, :] <= positions[:, None]) & (positions[None, :] < valid_len)
    normed_in, norm_back_in = jax.vjp(gain_norm, inputs, gain_attn.astype(jnp.float32))
    in_low = normed_in.astype(jnp.bfloat16)
    query_pre = low_dot(in_low, w_query)
    key_pre = low_dot(in_low, w_key)
    value_pre = low_dot(in_low, w_value)
    outgate_pre = low_dot(in_low, w_outgate)
    forget_pre = low_dot(in_low, w_forget) + b_forget.astype(jnp.float32)
    query_norm, query_back = jax.vjp(norm_rows, query_pre.reshape(seq_len, head_count, head_dim))
    key_norm, key_back = jax.vjp(norm_rows, key_pre.reshape(seq_len, head_count, head_dim))
    query_low = query_norm.astype(jnp.bfloat16)
    key_low = key_norm.astype(jnp.bfloat16)
    value_low = value_pre.astype(jnp.bfloat16).reshape(seq_len, head_count, head_dim)
    log_decay = jnp.cumsum(jax.nn.log_sigmoid(forget_pre), axis=0).T

    def masked_scores():
        base_scores = (
            jnp.einsum("ihd,jhd->hij", query_low, key_low, preferred_element_type=jnp.float32)
            * score_scale
        )
        base_scores = base_scores + log_decay[:, :, None] - log_decay[:, None, :]
        return jnp.where(allowed[None], base_scores, -1e30)

    masked = masked_scores()
    row_top = jnp.max(masked, axis=-1, keepdims=True)
    exponent = jnp.exp(masked - row_top)
    row_total = jnp.sum(exponent, axis=-1, keepdims=True)
    attn_probs = exponent / row_total
    log_total = row_top + jnp.log(row_total)
    attended = jnp.einsum(
        "hij,jhd->ihd",
        attn_probs.astype(jnp.bfloat16),
        value_low,
        preferred_element_type=jnp.float32,
    ).reshape(seq_len, head_count * head_dim)
    gate_sig = jax.nn.sigmoid(outgate_pre)
    gated_low = (attended * gate_sig).astype(jnp.bfloat16)
    branch_attn = lax.psum(low_dot(gated_low, w_out), "mp")
    middle = inputs + branch_attn
    normed_mid, norm_back_mid = jax.vjp(gain_norm, middle, gain_mlp.astype(jnp.float32))
    mid_low = normed_mid.astype(jnp.bfloat16)
    gate_pre = low_dot(mid_low, w_gate)
    up_pre = low_dot(mid_low, w_up)
    hidden_f, swiglu_back = jax.vjp(swiglu, gate_pre, up_pre)
    hidden_low = hidden_f.astype(jnp.bfloat16)
    branch_mlp = lax.psum(low_dot(hidden_low, w_down), "mp")
    layer_out = (middle + branch_mlp).astype(jnp.bfloat16)
    bucket_hot = (buckets[0] == jnp.arange(NBUCKET)).astype(jnp.float32)
    square_sums = jnp.stack(
        [
            jnp.sum(valid_rows * inputs * inputs),
            jnp.sum(valid_rows * branch_attn * branch_attn),
            jnp.sum(valid_rows * branch_mlp * branch_mlp),
        ]
    )
    bucket_sums = square_sums[:, None] * bucket_hot[None, :]
    bucket_count = valid_len.astype(jnp.float32) * bucket_hot
    grad_rows = out_cotangent[0].astype(jnp.float32) * valid_rows
    grad_rows_low = grad_rows.astype(jnp.bfloat16)
    grad_w_down = back_dot(hidden_low, grad_rows_low)
    grad_hidden = trans_dot(grad_rows_low, w_down)
    grad_gate_f, grad_up_f = swiglu_back(grad_hidden)
    gate_grad_low = grad_gate_f.astype(jnp.bfloat16)
    up_grad_low = grad_up_f.astype(jnp.bfloat16)
    grad_w_gate = back_dot(mid_low, gate_grad_low)
    grad_w_up = back_dot(mid_low, up_grad_low)
    grad_mid_norm = lax.psum(trans_dot(gate_grad_low, w_gate) + trans_dot(up_grad_low, w_up), "mp")
    grad_middle_part, grad_gain_mlp = norm_back_mid(grad_mid_norm)
    grad_middle = grad_rows + grad_middle_part
    middle_low = grad_middle.astype(jnp.bfloat16)
    grad_w_out = back_dot(gated_low, middle_low)
    grad_gated = trans_dot(middle_low, w_out)
    attended_grad_low = (grad_gated * gate_sig).astype(jnp.bfloat16)
    outgate_grad_low = (grad_gated * attended * gate_sig * (1.0 - gate_sig)).astype(jnp.bfloat16)
    attended_heads = attended_grad_low.reshape(seq_len, head_count, head_dim)
    again_probs = jnp.exp(masked_scores() - log_total)
    grad_probs = jnp.einsum(
        "ihd,jhd->hij", attended_heads, value_low, preferred_element_type=jnp.float32
    )
    row_delta = jnp.sum(again_probs * grad_probs, axis=-1, keepdims=True)
    scores_grad_low = (again_probs * (grad_probs - row_delta)).astype(jnp.bfloat16)
    value_grad_low = (
        jnp.einsum(
            "hij,ihd->jhd",
            again_probs.astype(jnp.bfloat16),
            attended_heads,
            preferred_element_type=jnp.float32,
        )
        .reshape(seq_len, head_count * head_dim)
        .astype(jnp.bfloat16)
    )
    grad_query_norm = (
        jnp.einsum("hij,jhd->ihd", scores_grad_low, key_low, preferred_element_type=jnp.float32)
        * score_scale
    )
    grad_key_norm = (
        jnp.einsum("hij,ihd->jhd", scores_grad_low, query_low, preferred_element_type=jnp.float32)
        * score_scale
    )
    score_grad = scores_grad_low.astype(jnp.float32)
    grad_decay = jnp.sum(score_grad, axis=2) - jnp.sum(score_grad, axis=1)
    grad_log_forget = jnp.flip(jnp.cumsum(jnp.flip(grad_decay, 1), axis=1), 1).T
    forget_grad_low = (grad_log_forget * jax.nn.sigmoid(-forget_pre)).astype(jnp.bfloat16)
    query_grad_low = (
        query_back(grad_query_norm)[0].reshape(seq_len, head_count * head_dim).astype(jnp.bfloat16)
    )
    key_grad_low = (
        key_back(grad_key_norm)[0].reshape(seq_len, head_count * head_dim).astype(jnp.bfloat16)
    )
    grad_w_query = back_dot(in_low, query_grad_low)
    grad_w_key = back_dot(in_low, key_grad_low)
    grad_w_value = back_dot(in_low, value_grad_low)
    grad_w_outgate = back_dot(in_low, outgate_grad_low)
    grad_w_forget = back_dot(in_low, forget_grad_low)
    grad_b_forget = jnp.sum(forget_grad_low.astype(jnp.float32), axis=0)
    grad_in_local = (
        trans_dot(query_grad_low, w_query)
        + trans_dot(key_grad_low, w_key)
        + trans_dot(value_grad_low, w_value)
    )
    grad_in_local = (
        grad_in_local
        + trans_dot(outgate_grad_low, w_outgate)
        + trans_dot(forget_grad_low, w_forget)
    )
    grad_in_norm = lax.psum(grad_in_local, "mp")
    grad_in_part, grad_gain_attn = norm_back_in(grad_in_norm)
    input_grad = grad_middle + grad_in_part
    all_shares = (
        *sent_together(
            (grad_gain_attn, grad_w_query, grad_w_key, grad_w_value, grad_w_outgate, grad_w_forget),
            "dp",
            0,
            1,
        ),
        lax.psum_scatter(grad_w_out, "dp", scatter_dimension=1, tiled=True),
        *side_by_side((grad_w_gate, grad_w_up), "dp", 0, 1),
        lax.psum_scatter(grad_w_down, "dp", scatter_dimension=1, tiled=True),
        lax.psum_scatter(grad_gain_mlp, "dp", scatter_dimension=0, tiled=True),
    )
    attn_shares = all_shares[:7]
    mlp_shares = all_shares[7:]
    bucket_total, bucket_rows, bias_sum = in_one((bucket_sums, bucket_count, grad_b_forget), "dp")
    rms = jnp.sqrt(bucket_total / (bucket_rows[None, :] * model_width))
    return (
        layer_out[None],
        input_grad[None],
        attn_shares[0],
        attn_shares[1],
        attn_shares[2],
        attn_shares[3],
        attn_shares[4],
        attn_shares[5],
        bias_sum,
        attn_shares[6],
        mlp_shares[3],
        mlp_shares[0],
        mlp_shares[1],
        mlp_shares[2],
        rms,
    )


def solution(mesh):
    placed = (
        P("dp", None, None),
        P("dp"),
        P("dp"),
        P("dp", None, None),
        P(),
        P(None, "mp"),
        P(None, "mp"),
        P(None, "mp"),
        P(None, "mp"),
        P(None, "mp"),
        P("mp"),
        P("mp", None),
        P(),
        P(None, "mp"),
        P(None, "mp"),
        P("mp", None),
    )
    return jax.shard_map(
        per_device,
        mesh=mesh,
        in_specs=placed,
        out_specs=(
            P("dp", None, None),
            P("dp", None, None),
            P("dp"),
            P("dp", "mp"),
            P("dp", "mp"),
            P("dp", "mp"),
            P("dp", "mp"),
            P("dp", "mp"),
            P("mp"),
            P("mp", "dp"),
            P("dp"),
            P("dp", "mp"),
            P("dp", "mp"),
            P("mp", "dp"),
            P(),
        ),
        check_vma=False,
    )
```

profile of v0, /device:TPU:0, one launch (start us, length us, event | category | flops | bytes accessed | tf_op | source)
XLA Modules:
  0.0 918.8 jit_solution(12748875508411315006)
XLA Ops:
  30.5 7.2 fusion.82
  37.6 6.9 fusion
  44.6 6.5 fusion.5
  58.5 103.3 %all-reduce.6.cloned.1.call-done = f32[768,1536]{1,0:T(8,128)} async-done(((f32[768,1536]{1,0:T(8,128)}), f32[768,1536]{1,0:T(8,128)}) %all-reduce.6.cloned.1.call-update) | async-done | bytes 4718608 | tf_op jit(solution)/shard_map/psum | solution.py:142
  187.1 5.6 fusion.86
  192.7 95.3 %all-reduce.8.cloned.1.call-done = f32[768,1536]{1,0:T(8,128)} async-done(((f32[768,1536]{1,0:T(8,128)}), f32[768,1536]{1,0:T(8,128)}) %all-reduce.8.cloned.1.call-update) | async-done | bytes 4718608 | tf_op jit(solution)/shard_map/psum | solution.py:171
  303.5 6.5 multiply_reduce_fusion
  310.1 9.8 %convert_reduce_fusion = (f32[6,768]{1,0:T(8,128)S(1)}, f32[6,768]{1,0:T(8,128)S(1)}, bf16[6,768,768]{1,2,0:T(8,128)(2,1)}) fusion(f32[6,768,768]{1,2,0:T(8,128)} %get-tuple-element.151, f32[6,768]{1,0:T(8,128)S(1)} %get-tuple-element.150, f32[6,768,768]{1,2,0:T(8,128)S(1)} %bitcast.193, f32[6,768]{1,0:T(8,128)S(1)} %log_add_fusion), kind=kLoop, calls=%fused_computation | loop fusion | flops 24763392 | bytes 35463168 | tf_op jit(solution)/shard_map/reduce_sum | solution.py:205
  319.9 6.3 multiply_reduce_fusion.4
  326.1 5.3 multiply_reduce_fusion.5
  353.4 6.2 fusion.93
  364.2 10.5 %pad_maximum_fusion = f32[1536,2048]{0,1:T(8,128)} fusion(f32[1536,1024]{0,1:T(8,128)} %fusion.94, f32[1536,1024]{0,1:T(8,128)} %fusion.93), kind=kLoop, calls=%fused_computation.8 | loop fusion | flops 3145728 | bytes 25165824 | tf_op jit(solution)/shard_map/concatenate | solution.py:24
  374.7 12.7 %copy.111 = f32[1536,2048]{1,0:T(8,128)} copy(f32[1536,2048]{0,1:T(8,128)} %pad_maximum_fusion) | data formatting | bytes 25165824
  401.1 128.1 %all-reduce.10.cloned.1.call-done = (f32[768,1536]{1,0:T(8,128)}, f32[768,1536]{1,0:T(8,128)}) async-done(((f32[768,1536]{1,0:T(8,128)}, f32[768,1536]{1,0:T(8,128)}), (f32[768,1536]{1,0:T(8,128)}, f32[768,1536]{1,0:T(8,128)})) %all-reduce.10.cloned.1.call-update) | async-done | bytes 9437200 | tf_op jit(solution)/shard_map/psum | solution.py:150
  529.3 10.4 %fusion.23 = (f32[]{:T(128)}, f32[]{:T(128)}, bf16[1,768,1536]{2,1,0:T(8,128)(2,1)}, f32[]{:T(128)}, f32[768]{0:T(1024)S(1)}, /*index=5*/f32[1536]{0:T(1024)S(1)}) fusion(f32[768,1536]{1,0:T(8,128)} %all-reduce.6.cloned.1.call-done, f32[768]{0:T(1024)S(1)} %fusion.72, f32[768,1536]{1,0:T(8,128)} %get-tuple-element.114, f32[768,1536]{1,0:T(8,128)} %copy-done.2, ...), kind=kLoop, calls=%fused_computation.39 | loop fusion | flops 21231356 | bytes 23614476 | tf_op jit(solution)/shard_map/reduce_sum | solution.py:156
  539.7 34.5 %concatenate.9 = f32[1536,1543]{0,1:T(8,128)} concatenate(f32[1536,1]{0,1:T(1,128)S(1)} %reshape.318, f32[1536,384]{0,1:T(8,128)} %fusion.37, f32[1536,384]{0,1:T(8,128)} %fusion.39, f32[1536,384]{0,1:T(8,128)} %fusion.35, f32[1536,384]{0,1:T(8,128)} %fusion.95, f32[1536,6]{0,1:T(8,128)S(1)} %fusion.92), dimensions={1} | concatenate | bytes 18960384 | tf_op jit(solution)/shard_map/concatenate | solution.py:13
  574.2 10.6 %copy.109 = f32[1536,1543]{1,0:T(8,128)} copy(f32[1536,1543]{0,1:T(8,128)} %concatenate.9) | data formatting | bytes 18960384
  586.0 5.3 fusion.54
  591.4 6.2 fusion.58
  599.5 69.3 %all-reduce = f32[1536]{0:T(1024)S(1)} all-reduce(f32[1536]{0:T(1024)S(1)} %get-tuple-element.105), channel_id=4, replica_groups=mesh['dp'=32,'mp'=4] {'dp'}, use_global_device_ids=true, to_apply=%region_30.31.clone | all-reduce | flops 1536 | bytes 12288
  676.2 8.4 fusion.21
  687.8 50.7 %reduce-scatter.13.cloned.1.call-done = f32[48,1543]{1,0:T(8,128)} async-done(((f32[1536,1543]{1,0:T(8,128)}), f32[48,1543]{1,0:T(8,128)}) %reduce-scatter.13.cloned.1.call-update) | async-done | bytes 296272
  743.2 78.4 %reduce-scatter.9.cloned.1.call-done = f32[384,48]{0,1:T(8,128)} async-done(((f32[384,1536]{0,1:T(8,128)}), f32[384,48]{0,1:T(8,128)}) %reduce-scatter.9.cloned.1.call-update) | async-done | bytes 73744 | tf_op jit(solution)/shard_map/reduce_scatter | solution.py:240
  821.5 90.0 %reduce-scatter.11.cloned.1.call-done = f32[1024,48]{0,1:T(8,128)} async-done(((f32[1024,1536]{0,1:T(8,128)}), f32[1024,48]{0,1:T(8,128)}) %reduce-scatter.11.cloned.1.call-update) | async-done | bytes 196624 | tf_op jit(solution)/shard_map/reduce_scatter | solution.py:242
  (223 shorter events, 127.6 us)
Async XLA Ops:
  7.2 167.4 %copy-start = (bf16[1024,1536]{1,0:T(8,128)(2,1)S(1)}, bf16[1024,1536]{1,0:T(8,128)(2,1)}, u32[]{:S(2)}) copy-start(bf16[1024,1536]{1,0:T(8,128)(2,1)} %param.31) | copy-start | bytes 9437188
  7.2 154.6 %all-reduce.6.cloned.1.call-start = ((), (), s32[]{:S(2)}) async-start(), calls=%async_computation.5 | async-start | bytes 9437184 | tf_op jit(solution)/shard_map/psum | solution.py:142
  9.6 15.2 %copy-start.45 = (f32[768]{0:T(1024)}, f32[768]{0:T(1024)S(1)}, u32[]{:S(2)}) copy-start(f32[768]{0:T(1024)S(1)} %fusion.70) | copy-start | bytes 9220
  10.3 14.5 %copy-start.42 = (f32[1536]{0:T(1024)}, f32[1536]{0:T(1024)S(1)}, u32[]{:S(2)}) copy-start(f32[1536]{0:T(1024)S(1)} %convert_element_type.141) | copy-start | bytes 18436
  30.3 14.2 %copy-start.40 = (bf16[768,384]{0,1:T(8,128)(2,1)}, bf16[768,384]{0,1:T(8,128)(2,1)S(1)}, u32[]{:S(2)}) copy-start(bf16[768,384]{0,1:T(8,128)(2,1)S(1)} %convolution_convert_fusion) | copy-start | bytes 1769476
  44.6 6.5 copy-start.38
  57.9 230.1 %all-reduce.8.cloned.1.call-start = ((), (), s32[]{:S(2)}) async-start(), calls=%async_computation.6 | async-start | bytes 9437184 | tf_op jit(solution)/shard_map/psum | solution.py:171
  186.6 342.6 %all-reduce.10.cloned.1.call-start = ((), (), s32[]{:S(2)}) async-start(), calls=%async_computation.11 | async-start | bytes 18874368 | tf_op jit(solution)/shard_map/psum | solution.py:150
  288.0 5.9 copy-start.29
  293.9 6.4 slice-start
  293.9 7.8 slice-start.1
  293.9 9.0 slice-start.2
  297.6 5.9 copy-start.41
  310.1 9.8 %copy-start.12 = (f32[768,6,64]{0,2,1:T(8,128)S(1)}, f32[768,6,64]{0,2,1:T(8,128)}, u32[]{:S(2)}) copy-start(f32[768,6,64]{0,2,1:T(8,128)} %get-tuple-element.143) | copy-start | bytes 3538948
  310.1 9.8 %copy-start.14 = (f32[768,6,64]{0,2,1:T(8,128)S(1)}, f32[768,6,64]{0,2,1:T(8,128)}, u32[]{:S(2)}) copy-start(f32[768,6,64]{0,2,1:T(8,128)} %copy-done.13) | copy-start | bytes 3538948
  351.7 334.3 %reduce-scatter.15.cloned.1.call-start = ((), (), s32[]{:S(2)}) async-start(), calls=%async_computation.10 | async-start | bytes 12976128
  353.4 6.2 copy-start.54
  387.4 351.1 %reduce-scatter.13.cloned.1.call-start = ((), (), s32[]{:S(2)}) async-start(), calls=%async_computation.9 | async-start | bytes 10543104
  584.8 6.6 copy-start.30
  584.8 236.7 %reduce-scatter.9.cloned.1.call-start = ((), (), s32[]{:S(2)}) async-start(), calls=%async_computation.7 | async-start | bytes 2433024 | tf_op jit(solution)/shard_map/reduce_scatter | solution.py:240
  591.3 320.2 %reduce-scatter.11.cloned.1.call-start = ((), (), s32[]{:S(2)}) async-start(), calls=%async_computation.8 | async-start | bytes 6488064 | tf_op jit(solution)/shard_map/reduce_scatter | solution.py:242
  597.6 78.6 %copy-start.48 = (f32[768]{0:T(1024)S(1)}, f32[768]{0:T(1024)}, u32[]{:S(2)}) copy-start(f32[768]{0:T(1024)} %copy-done.47) | copy-start | bytes 9220
  672.3 12.3 %all-to-all-start = ((f32[32,1,22]{2,1,0:T(1,128)}), f32[32,1,22]{2,1,0:T(1,128)S(1)}, u32[]{:S(2)}, u32[]{:S(2)}) async-start(f32[32,1,22]{2,1,0:T(1,128)} %broadcast_in_dim.38), calls=%async_computation | async-start | bytes 32768 | tf_op jit(solution)/shard_map/all_to_all | solution.py:34
  676.2 235.4 %copy-start.1 = (bf16[1024,1536]{1,0:T(8,128)(2,1)S(1)}, bf16[1024,1536]{1,0:T(8,128)(2,1)}, u32[]{:S(2)}) copy-start(bf16[1024,1536]{1,0:T(8,128)(2,1)} %param.31) | copy-start | bytes 9437188
  (44 other events, 113.7 us)
Sparse Core Ops, SparseCore 0:
  58.0 103.7 all-reduce.5
  186.7 101.2 all-reduce.7
  351.9 177.3 all-reduce.9
  533.0 104.4 reduce-scatter.14
  641.6 96.8 reduce-scatter.12
  742.9 78.5 reduce-scatter.8
  825.9 85.6 reduce-scatter.10
where the time goes:
time: 930 us; the launch traced here: 919 us
  waiting for transfers between devices  546 us (59%)
  matrix products  119 us (13%)
  local copies, waits for them, and re-layouts  90.5 us (10%)
  other arithmetic  72.1 us (8%)
  blocking collectives  69.3 us (7%)
  between operations  17.2 us (2%)
    psum x1, waiting for transfers between devices, per_device(): branch_mlp = lax.psum(low_dot(hidden_low, w_down), 'mp')  128 us
    psum x1, waiting for transfers between devices, per_device(): branch_attn = lax.psum(low_dot(gated_low, w_out), 'mp')  103 us
    psum x1, waiting for transfers between devices, per_device(): lax.psum(trans_dot(gate_grad_low, w_gate) + trans_dot(up_grad_low, w_up),...  95.3 us
    reduce_scatter x1, waiting for transfers between devices, per_device(): lax.psum_scatter(grad_w_down, 'dp', scatter_dimension=1, tiled=True)  90 us
    reduce_scatter x1, waiting for transfers between devices, per_device(): lax.psum_scatter(grad_w_out, 'dp', scatter_dimension=1, tiled=True)  78.4 us
    unnamed x1, blocking collectives  69.3 us
    unnamed x9, waiting for transfers between devices  50.8 us
    unnamed x130, local copies, waits for them, and re-layouts  48 us
  transfers between devices with their start and end apart: 8, of which 6 were waited for; matrix products, arithmetic and copies ran while one was open for 15% of the time, Pallas kernels for 0%

commit v1 on v0

--- a/solution.py
+++ b/solution.py
@@ -139,7 +139,7 @@
     ).reshape(seq_len, head_count * head_dim)
     gate_sig = jax.nn.sigmoid(outgate_pre)
     gated_low = (attended * gate_sig).astype(jnp.bfloat16)
-    branch_attn = lax.psum(low_dot(gated_low, w_out), "mp")
+    branch_attn = jnp.sum(lax.all_gather(low_dot(gated_low, w_out), "mp"), axis=0)
     middle = inputs + branch_attn
     normed_mid, norm_back_mid = jax.vjp(gain_norm, middle, gain_mlp.astype(jnp.float32))
     mid_low = normed_mid.astype(jnp.bfloat16)

time: 930 us -> 1010 us (1.086)
  waiting for transfers between devices: 546 us -> 617 us
  other arithmetic: 72.1 us -> 83.4 us
    all_gather x0 -> x1, waiting for transfers between devices: none -> 174 us  [per_device(): lax.all_gather(low_dot(gated_low, w_out), 'mp')]
    psum x1 -> x0, waiting for transfers between devices: 103 us -> none  [per_device(): branch_attn = lax.psum(low_dot(gated_low, w_out), 'mp')]
    reduce_sum x0 -> x1, other arithmetic: none -> 11.3 us  [per_device(): jnp.sum(lax.all_gather(low_dot(gated_low, w_out), 'mp'), axis=0)]
  transfers between devices with their start and end apart: 8 -> 8, of which waited for: 6 -> 6; matrix products, arithmetic and copies ran while one was open for 15% -> 14% of each run, Pallas kernels for 0% -> 0%
where the time goes in v1:
time: 1010 us; the launch traced here: 1000 us
  waiting for transfers between devices  617 us (61%)
  matrix products  119 us (12%)
  local copies, waits for them, and re-layouts  90.3 us (9%)
  other arithmetic  83.4 us (8%)
  blocking collectives  69.4 us (7%)
  between operations  17.3 us (2%)
    all_gather x1, waiting for transfers between devices, per_device(): lax.all_gather(low_dot(gated_low, w_out), 'mp')  174 us
    psum x1, waiting for transfers between devices, per_device(): branch_mlp = lax.psum(low_dot(hidden_low, w_down), 'mp')  128 us
    psum x1, waiting for transfers between devices, per_device(): lax.psum(trans_dot(gate_grad_low, w_gate) + trans_dot(up_grad_low, w_up),...  95.6 us
    reduce_scatter x1, waiting for transfers between devices, per_device(): lax.psum_scatter(grad_w_down, 'dp', scatter_dimension=1, tiled=True)  90 us
    reduce_scatter x1, waiting for transfers between devices, per_device(): lax.psum_scatter(grad_w_out, 'dp', scatter_dimension=1, tiled=True)  78.4 us
    unnamed x1, blocking collectives  69.4 us
    unnamed x9, waiting for transfers between devices  50.6 us
    unnamed x130, local copies, waits for them, and re-layouts  47.9 us
  transfers between devices with their start and end apart: 8, of which 6 were waited for; matrix products, arithmetic and copies ran while one was open for 14% of the time, Pallas kernels for 0%

profile of v1, /device:TPU:0, one launch (start us, length us, event | category | flops | bytes accessed | tf_op | source)
XLA Modules:
  0.0 1001.5 jit_solution(9092036079717061158)
XLA Ops:
  30.5 7.3 fusion.82
  37.7 6.9 fusion
  44.7 6.5 fusion.5
  58.6 174.4 %all-gather.3.cloned.1.call-done = f32[3072,1536]{1,0:T(8,128)} async-done(((f32[768,1536]{1,0:T(8,128)}), f32[3072,1536]{1,0:T(8,128)}) %all-gather.3.cloned.1.call-update) | async-done | bytes 18874384 | tf_op jit(solution)/shard_map/all_gather | solution.py:142
  233.0 11.3 %reduce_sum.208 = f32[768,1536]{1,0:T(8,128)} reduce(f32[4,768,1536]{2,1,0:T(8,128)} %bitcast.194, f32[]{:T(128)} %constant.18.clone.1), dimensions={0}, to_apply=%region_7.8 | reduce | flops 3538944 | bytes 23592964 | tf_op jit(solution)/shard_map/reduce_sum | solution.py:142
  269.2 5.8 fusion.86
  275.0 95.6 %all-reduce.5.cloned.1.call-done = f32[768,1536]{1,0:T(8,128)} async-done(((f32[768,1536]{1,0:T(8,128)}), f32[768,1536]{1,0:T(8,128)}) %all-reduce.5.cloned.1.call-update) | async-done | bytes 4718608 | tf_op jit(solution)/shard_map/psum | solution.py:171
  386.2 6.5 multiply_reduce_fusion
  392.7 9.8 convert_reduce_fusion
  402.5 6.3 multiply_reduce_fusion.4
  408.8 5.3 multiply_reduce_fusion.5
  436.1 6.2 fusion.93
  447.0 10.4 %pad_maximum_fusion = f32[1536,2048]{0,1:T(8,128)} fusion(f32[1536,1024]{0,1:T(8,128)} %fusion.94, f32[1536,1024]{0,1:T(8,128)} %fusion.93), kind=kLoop, calls=%fused_computation.8 | loop fusion | flops 3145728 | bytes 25165824 | tf_op jit(solution)/shard_map/concatenate | solution.py:24
  457.4 12.7 %copy.111 = f32[1536,2048]{1,0:T(8,128)} copy(f32[1536,2048]{0,1:T(8,128)} %pad_maximum_fusion) | data formatting | bytes 25165824
  483.9 128.1 %all-reduce.7.cloned.1.call-done = (f32[768,1536]{1,0:T(8,128)}, f32[768,1536]{1,0:T(8,128)}) async-done(((f32[768,1536]{1,0:T(8,128)}, f32[768,1536]{1,0:T(8,128)}), (f32[768,1536]{1,0:T(8,128)}, f32[768,1536]{1,0:T(8,128)})) %all-reduce.7.cloned.1.call-update) | async-done | bytes 9437200 | tf_op jit(solution)/shard_map/psum | solution.py:150
  612.0 10.4 %fusion.23 = (f32[]{:T(128)}, f32[]{:T(128)}, bf16[1,768,1536]{2,1,0:T(8,128)(2,1)}, f32[]{:T(128)}, f32[768]{0:T(1024)S(1)}, /*index=5*/f32[1536]{0:T(1024)S(1)}) fusion(f32[768,1536]{1,0:T(8,128)} %reduce_sum.208, f32[768]{0:T(1024)S(1)} %get-tuple-element.157, f32[768,1536]{1,0:T(8,128)} %get-tuple-element.114, f32[768,1536]{1,0:T(8,128)} %copy-done.2, ...), kind=kLoop, calls=%fused_computation.39 | loop fusion | flops 21231356 | bytes 23614476 | tf_op jit(solution)/shard_map/reduce_sum | solution.py:156
  622.4 34.5 %concatenate.9 = f32[1536,1543]{0,1:T(8,128)} concatenate(f32[1536,1]{0,1:T(1,128)S(1)} %reshape.318, f32[1536,384]{0,1:T(8,128)} %fusion.37, f32[1536,384]{0,1:T(8,128)} %fusion.39, f32[1536,384]{0,1:T(8,128)} %fusion.35, f32[1536,384]{0,1:T(8,128)} %fusion.95, f32[1536,6]{0,1:T(8,128)S(1)} %fusion.92), dimensions={1} | concatenate | bytes 18960384 | tf_op jit(solution)/shard_map/concatenate | solution.py:13
  656.9 10.7 %copy.109 = f32[1536,1543]{1,0:T(8,128)} copy(f32[1536,1543]{0,1:T(8,128)} %concatenate.9) | data formatting | bytes 18960384
  674.1 6.3 fusion.58
  682.4 69.4 %all-reduce = f32[1536]{0:T(1024)S(1)} all-reduce(f32[1536]{0:T(1024)S(1)} %get-tuple-element.105), channel_id=5, replica_groups=mesh['dp'=32,'mp'=4] {'dp'}, use_global_device_ids=true, to_apply=%region_30.31.clone | all-reduce | flops 1536 | bytes 12288
  759.1 8.4 fusion.21
  770.7 50.5 %reduce-scatter.13.cloned.1.call-done = f32[48,1543]{1,0:T(8,128)} async-done(((f32[1536,1543]{1,0:T(8,128)}), f32[48,1543]{1,0:T(8,128)}) %reduce-scatter.13.cloned.1.call-update) | async-done | bytes 296272
  825.8 78.4 %reduce-scatter.9.cloned.1.call-done = f32[384,48]{0,1:T(8,128)} async-done(((f32[384,1536]{0,1:T(8,128)}), f32[384,48]{0,1:T(8,128)}) %reduce-scatter.9.cloned.1.call-update) | async-done | bytes 73744 | tf_op jit(solution)/shard_map/reduce_scatter | solution.py:240
  904.2 90.0 %reduce-scatter.11.cloned.1.call-done = f32[1024,48]{0,1:T(8,128)} async-done(((f32[1024,1536]{0,1:T(8,128)}), f32[1024,48]{0,1:T(8,128)}) %reduce-scatter.11.cloned.1.call-update) | async-done | bytes 196624 | tf_op jit(solution)/shard_map/reduce_scatter | solution.py:242
  (223 shorter events, 132.6 us)
Async XLA Ops:
  7.2 249.9 %copy-start = (bf16[1024,1536]{1,0:T(8,128)(2,1)S(1)}, bf16[1024,1536]{1,0:T(8,128)(2,1)}, u32[]{:S(2)}) copy-start(bf16[1024,1536]{1,0:T(8,128)(2,1)} %param.31) | copy-start | bytes 9437188
  7.2 225.8 %all-gather.3.cloned.1.call-start = ((), (), s32[]{:S(2)}) async-start(), calls=%async_computation.8 | async-start | bytes 23592960 | tf_op jit(solution)/shard_map/all_gather | solution.py:142
  9.6 15.2 %copy-start.45 = (f32[768]{0:T(1024)}, f32[768]{0:T(1024)S(1)}, u32[]{:S(2)}) copy-start(f32[768]{0:T(1024)S(1)} %fusion.70) | copy-start | bytes 9220
  10.3 14.5 %copy-start.42 = (f32[1536]{0:T(1024)}, f32[1536]{0:T(1024)S(1)}, u32[]{:S(2)}) copy-start(f32[1536]{0:T(1024)S(1)} %convert_element_type.141) | copy-start | bytes 18436
  30.3 14.3 %copy-start.40 = (bf16[768,384]{0,1:T(8,128)(2,1)}, bf16[768,384]{0,1:T(8,128)(2,1)S(1)}, u32[]{:S(2)}) copy-start(bf16[768,384]{0,1:T(8,128)(2,1)S(1)} %convolution_convert_fusion) | copy-start | bytes 1769476
  44.7 6.5 copy-start.38
  58.0 312.7 %all-reduce.5.cloned.1.call-start = ((), (), s32[]{:S(2)}) async-start(), calls=%async_computation.5 | async-start | bytes 9437184 | tf_op jit(solution)/shard_map/psum | solution.py:171
  269.1 342.9 %all-reduce.7.cloned.1.call-start = ((), (), s32[]{:S(2)}) async-start(), calls=%async_computation.11 | async-start | bytes 18874368 | tf_op jit(solution)/shard_map/psum | solution.py:150
  370.6 5.9 copy-start.29
  376.5 6.4 slice-start
  376.5 7.8 slice-start.1
  376.5 9.0 slice-start.2
  380.2 5.9 copy-start.41
  392.7 9.8 copy-start.12
  392.7 9.8 copy-start.14
  434.5 334.4 %reduce-scatter.15.cloned.1.call-start = ((), (), s32[]{:S(2)}) async-start(), calls=%async_computation.10 | async-start | bytes 12976128
  436.1 6.2 copy-start.54
  470.1 351.0 %reduce-scatter.13.cloned.1.call-start = ((), (), s32[]{:S(2)}) async-start(), calls=%async_computation.9 | async-start | bytes 10543104
  667.5 6.5 copy-start.30
  667.6 236.6 %reduce-scatter.9.cloned.1.call-start = ((), (), s32[]{:S(2)}) async-start(), calls=%async_computation.6 | async-start | bytes 2433024 | tf_op jit(solution)/shard_map/reduce_scatter | solution.py:240
  674.0 320.2 %reduce-scatter.11.cloned.1.call-start = ((), (), s32[]{:S(2)}) async-start(), calls=%async_computation.7 | async-start | bytes 6488064 | tf_op jit(solution)/shard_map/reduce_scatter | solution.py:242
  680.4 78.7 %copy-start.48 = (f32[768]{0:T(1024)S(1)}, f32[768]{0:T(1024)}, u32[]{:S(2)}) copy-start(f32[768]{0:T(1024)} %copy-done.47) | copy-start | bytes 9220
  755.2 12.3 %all-to-all-start = ((f32[32,1,22]{2,1,0:T(1,128)}), f32[32,1,22]{2,1,0:T(1,128)S(1)}, u32[]{:S(2)}, u32[]{:S(2)}) async-start(f32[32,1,22]{2,1,0:T(1,128)} %broadcast_in_dim.38), calls=%async_computation | async-start | bytes 32768 | tf_op jit(solution)/shard_map/all_to_all | solution.py:34
  759.1 235.1 %copy-start.1 = (bf16[1024,1536]{1,0:T(8,128)(2,1)S(1)}, bf16[1024,1536]{1,0:T(8,128)(2,1)}, u32[]{:S(2)}) copy-start(bf16[1024,1536]{1,0:T(8,128)(2,1)} %param.31) | copy-start | bytes 9437188
  (44 other events, 113.9 us)
Sparse Core Ops, SparseCore 0:
  58.1 174.8 all-gather.2
  269.2 101.3 all-reduce.4
  434.6 177.3 all-reduce.6
  615.7 104.4 reduce-scatter.14
  724.4 96.7 reduce-scatter.12
  825.5 78.5 reduce-scatter.8
  908.5 85.6 reduce-scatter.10
